TPU v7x, 32 devices: a whole 2x2x4 slice. The times are simulated.
32 devices in a mesh: dp: 8 (over z, x), mp: 4 (over y, core).
Axes of the slice: x: 2, y: 2, z: 4, core: 2. Of those that a mesh axis runs over, the one named last changes fastest.
Arguments:
- patches: bfloat16 [9216, 3072], P('dp'), may hold values from -6 to 6
- weight: bfloat16 [3072, 1536], P(None, 'mp'), may hold values from -0.109375 to 0.109375
- conv_bias: float32 [1536], P('mp'), may hold values from -3 to 3
- cotangent: bfloat16 [9216, 1536], P('dp', 'mp'), may hold values from -0.0390625 to 0.0390625
- row_scale: float32 [3072], replicated, may hold values from 0.25 to 4
- col_scale: float32 [1536], P('mp'), may hold values from 0.25 to 4
Outputs:
- output: bfloat16 [9216, 1536], P('dp', 'mp')
- left_factor: float32 [3072, 3072], P('dp', 'mp')
- right_factor: float32 [1536, 1536], P('dp', 'mp')
- norm_pair: float32 [2], replicated
All inputs are finite; a program needn't handle non-finite values.
Results may differ from a plain program's by a relative error of at most 0.001.
Values sent between devices are 32-bit elements; how exact they have to be, the bound alone decides.
A program may use at most 64 MiB of HBM per device.

v0:
```python
import jax
import jax.numpy as jnp
from jax import lax
from jax.sharding import PartitionSpec as P

COUT = 1536
K = 3072


def shards(patches, weight, conv_bias, cotangent, row_scale, col_scale):
    output = (jnp.dot(patches, weight, preferred_element_type=jnp.float32) + conv_bias).astype(
        jnp.bfloat16
    )
    inner_width = patches.shape[1]
    strip_rows = inner_width // lax.axis_size("dp")
    local_grad = lax.dot_general(
        patches, cotangent, (((0,), (0,)), ((), ())), preferred_element_type=jnp.float32
    )
    weighted = local_grad * row_scale[:, None] * col_scale[None, :]
    small_sum = jnp.sum(weighted * weighted)
    column = lax.psum(local_grad, "dp")
    rows_here = lax.dynamic_slice_in_dim(column, lax.axis_index("dp") * strip_rows, strip_rows, 0)
    left_part = lax.dot_general(
        rows_here,
        column,
        (((1,), (1,)), ((), ())),
        precision=lax.Precision.HIGHEST,
        preferred_element_type=jnp.float32,
    )
    left_factor = lax.psum_scatter(left_part / COUT, "mp", scatter_dimension=1, tiled=True)
    full_strip = lax.all_gather(rows_here, "mp", axis=1, tiled=True)
    right_factor = lax.psum_scatter(
        lax.dot_general(
            full_strip,
            rows_here,
            (((0,), (0,)), ((), ())),
            precision=lax.Precision.HIGHEST,
            preferred_element_type=jnp.float32,
        )
        / K,
        "dp",
        scatter_dimension=0,
        tiled=True,
    )
    row_part = lax.dynamic_slice_in_dim(row_scale, lax.axis_index("dp") * strip_rows, strip_rows, 0)
    scaled_rows = rows_here * row_part[:, None] * col_scale[None, :]
    large_sum = jnp.sum(scaled_rows * scaled_rows)
    small_total, large_total = lax.psum((small_sum, large_sum), ("dp", "mp"))
    norm_pair = jnp.stack([small_total, large_total]) / (K * COUT)
    return (output, left_factor, right_factor, norm_pair)


def solution(mesh):
    in_specs = (P("dp", None), P(None, "mp"), P("mp"), P("dp", "mp"), P(), P("mp"))
    out_specs = (P("dp", "mp"), P("dp", "mp"), P("dp", "mp"), P())
    return jax.shard_map(shards, mesh=mesh, in_specs=in_specs, out_specs=out_specs, check_vma=False)
```

profile of v0, /device:TPU:0, one launch (start us, length us, event | category | flops | bytes accessed | tf_op | source)
XLA Modules:
  0.0 348.9 jit_solution(10241874328816004457)
XLA Ops:
  7.2 0.0 copy-start
  7.2 0.0 all-reduce.3.cloned.1.call-start
  7.2 10.4 %multiply_reduce_fusion = (f32[]{:T(128)}, f32[3072,384]{1,0:T(8,128)}) fusion(f32[384]{0:T(512)} %param.11, f32[3072]{0:T(1024)} %param.10, bf16[1152,3072]{1,0:T(8,128)(2,1)} %param.6, bf16[1152,384]{1,0:T(8,128)(2,1)} %param.9), kind=kOutput, calls=%fused_computation | convolution fusion | flops 2722627584 | bytes 12695044 | tf_op jit(solution)/shard_map/dot_general | solution.py:16
  17.6 0.0 copy-start.2
  17.6 0.0 all-reduce.3.cloned.1.call-update
  17.7 0.0 all-gather.2.cloned.1.call-start
  17.7 0.8 dynamic_slice.7
  18.5 171.7 %all-reduce.3.cloned.1.call-done = f32[3072,384]{1,0:T(8,128)} async-done(((f32[3072,384]{1,0:T(8,128)}), f32[3072,384]{1,0:T(8,128)}) %all-reduce.3.cloned.1.call-update) | async-done | bytes 4718608 | tf_op jit(solution)/shard_map/psum | solution.py:21
  190.2 0.0 copy-done.2
  190.2 2.6 multiply_reduce_fusion.1
  192.7 0.0 copy-start.1
  192.7 0.0 all-gather.2.cloned.1.call-update
  192.8 0.0 reduce-scatter.5.cloned.1.call-start
  192.8 23.2 %all-gather.2.cloned.1.call-done = f32[384,1536]{1,0:T(8,128)} async-done(((f32[384,384]{1,0:T(8,128)}), f32[384,1536]{1,0:T(8,128)}) %all-gather.2.cloned.1.call-update) | async-done | bytes 2359312 | tf_op jit(solution)/shard_map/all_gather | solution.py:31
  216.0 7.2 %convolution_multiply_fusion.1 = f32[1536,384]{1,0:T(8,128)} fusion(f32[384,1536]{1,0:T(8,128)} %all-gather.2.cloned.1.call-done, f32[384,384]{1,0:T(8,128)} %get-tuple-element.7), kind=kOutput, calls=%fused_computation.2 | convolution fusion | flops 2718498816 | bytes 5308416 | tf_op jit(solution)/shard_map/dot_general | solution.py:33
  223.3 0.0 reduce-scatter.5.cloned.1.call-update
  223.3 0.2 reduce-scatter.3.cloned.1.call-start
  223.5 0.0 copy-done.1
  223.5 11.0 %convolution_multiply_fusion = f32[384,3072]{1,0:T(8,128)} fusion(f32[384,384]{1,0:T(8,128)S(1)} %copy-done.1, f32[3072,384]{1,0:T(8,128)} %all-reduce.3.cloned.1.call-done), kind=kOutput, calls=%fused_computation.1 | convolution fusion | flops 5436997632 | bytes 10027008 | tf_op jit(solution)/shard_map/dot_general | solution.py:23
  234.5 0.0 copy-start.3
  234.5 0.0 reduce-scatter.3.cloned.1.call-update
  234.5 0.0 copy-done
  234.5 0.6 copy-done.3
  235.2 7.1 %fusion = bf16[1152,384]{1,0:T(8,128)(2,1)} fusion(bf16[1152,3072]{1,0:T(8,128)(2,1)} %param.6, bf16[3072,384]{1,0:T(8,128)(2,1)S(1)} %copy-done, f32[384]{0:T(512)S(1)} %copy-done.3), kind=kOutput, calls=%fused_computation.4 | convolution fusion | flops 2718793728 | bytes 10323456 | tf_op jit(solution)/shard_map/dot_general | solution.py:11
  242.2 39.6 %all-reduce = (f32[1]{0:T(128)}, f32[1]{0:T(128)}) all-reduce(f32[1]{0:T(128)} %bitcast.1, f32[1]{0:T(128)} %bitcast), channel_id=1, replica_groups=mesh['dp'=8,'mp'=4] {'dp','mp'}, use_global_device_ids=true, to_apply=%region_6.0 | all-reduce | flops 2 | bytes 16 | tf_op jit(solution)/shard_map/psum | solution.py:48
  281.8 1.8 maximum_multiply_fusion
  283.6 9.1 %reduce-scatter.5.cloned.1.call-done = f32[192,384]{1,0:T(8,128)} async-done(((f32[1536,384]{1,0:T(8,128)}), f32[192,384]{1,0:T(8,128)}) %reduce-scatter.5.cloned.1.call-update) | async-done | bytes 294928 | tf_op jit(solution)/shard_map/reduce_scatter | solution.py:32
  292.7 49.7 %reduce-scatter.3.cloned.1.call-done = f32[384,768]{1,0:T(8,128)} async-done(((f32[384,3072]{1,0:T(8,128)}), f32[384,768]{1,0:T(8,128)}) %reduce-scatter.3.cloned.1.call-update) | async-done | bytes 1179664 | tf_op jit(solution)/shard_map/reduce_scatter | solution.py:30
Async XLA Ops:
  7.2 227.3 %copy-start = (bf16[3072,384]{1,0:T(8,128)(2,1)S(1)}, bf16[3072,384]{1,0:T(8,128)(2,1)}, u32[]{:S(2)}) copy-start(bf16[3072,384]{1,0:T(8,128)(2,1)} %param.7) | copy-start | bytes 7077892
  7.2 183.0 %all-reduce.3.cloned.1.call-start = ((), (), s32[]{:S(2)}) async-start(), calls=%async_computation.2 | async-start | bytes 9437184 | tf_op jit(solution)/shard_map/psum | solution.py:21
  17.6 172.5 %copy-start.2 = (f32[384]{0:T(512)S(1)}, f32[384]{0:T(512)}, u32[]{:S(2)}) copy-start(f32[384]{0:T(512)} %param.11) | copy-start | bytes 4612
  17.7 198.3 %all-gather.2.cloned.1.call-start = ((), (), s32[]{:S(2)}) async-start(), calls=%async_computation.4 | async-start | bytes 2949120 | tf_op jit(solution)/shard_map/all_gather | solution.py:31
  192.7 30.8 %copy-start.1 = (f32[384,384]{1,0:T(8,128)S(1)}, f32[384,384]{1,0:T(8,128)}, u32[]{:S(2)}) copy-start(f32[384,384]{1,0:T(8,128)} %get-tuple-element.7) | copy-start | bytes 1769476
  192.8 99.9 %reduce-scatter.5.cloned.1.call-start = ((), (), s32[]{:S(2)}) async-start(), calls=%async_computation.5 | async-start | bytes 2654208 | tf_op jit(solution)/shard_map/reduce_scatter | solution.py:32
  223.3 119.1 %reduce-scatter.3.cloned.1.call-start = ((), (), s32[]{:S(2)}) async-start(), calls=%async_computation.3 | async-start | bytes 5898240 | tf_op jit(solution)/shard_map/reduce_scatter | solution.py:30
  234.5 0.7 copy-start.3
Sparse Core Ops, SparseCore 0:
  17.8 172.3 all-reduce.2
  192.9 23.0 all-gather.1
  223.4 69.2 reduce-scatter.4
  295.7 46.6 reduce-scatter.2
where the time goes:
time: 349 us
  waiting for transfers between devices  254 us (73%)
  blocking collectives  39.6 us (11%)
  matrix products  35.7 us (10%)
  between operations  13.8 us (4%)
  other arithmetic  4.38 us (1%)
    psum x1, waiting for transfers between devices, shards(): column = lax.psum(local_grad, 'dp')  172 us
    reduce_scatter x1, waiting for transfers between devices, shards(): lax.psum_scatter(left_part / COUT, 'mp', scatter_dimension=1, tiled=True)  49.7 us
    psum x1, blocking collectives, shards(): small_total, large_total = lax.psum((small_sum, large_sum), ('dp', 'mp'))  39.6 us
    all_gather x1, waiting for transfers between devices, shards(): full_strip = lax.all_gather(rows_here, 'mp', axis=1, tiled=True)  23.2 us
    dot_general x1, matrix products, shards(): lax.dot_general(rows_here, column, (((1,), (1,)), ((), ())), precision=la...  11 us
    dot_general x1, matrix products, shards(): lax.dot_general(patches, cotangent, (((0,), (0,)), ((), ())), preferred_e...  10.4 us
    reduce_scatter x1, waiting for transfers between devices, shards(): lax.psum_scatter(lax.dot_general(full_strip, rows_here, (((0,), (0,)), ((...  9.1 us
    dot_general x1, matrix products, shards(): lax.dot_general(full_strip, rows_here, (((0,), (0,)), ((), ())), precisio...  7.25 us
  transfers between devices with their start and end apart: 4, of which 4 were waited for; matrix products, arithmetic and copies ran while one was open for 6% of the time, Pallas kernels for 0%

commit v1 on v0

--- a/solution.py
+++ b/solution.py
@@ -1,3 +1,4 @@
+import functools
 import jax
 import jax.numpy as jnp
 from jax import lax
@@ -5,6 +6,14 @@
 
 COUT = 1536
 K = 3072
+
+
+def leaves_report(body, group_axis):
+    mat_out = jax.lax.all_gather(body, group_axis).sum(axis=0)
+    return mat_out
+
+
+lift_circles = functools.partial(leaves_report, group_axis="dp")
 
 
 def shards(patches, weight, conv_bias, cotangent, row_scale, col_scale):
@@ -18,7 +27,7 @@
     )
     weighted = local_grad * row_scale[:, None] * col_scale[None, :]
     small_sum = jnp.sum(weighted * weighted)
-    column = lax.psum(local_grad, "dp")
+    column = lift_circles(local_grad)
     rows_here = lax.dynamic_slice_in_dim(column, lax.axis_index("dp") * strip_rows, strip_rows, 0)
     left_part = lax.dot_general(
         rows_here,

time: 349 us -> 913 us (2.62)
  waiting for transfers between devices: 254 us -> 801 us
  other arithmetic: 4.38 us -> 20.3 us
    all_gather x0 -> x1, waiting for transfers between devices: none -> 718 us  [leaves_report(): mat_out = jax.lax.all_gather(body, group_axis).sum(axis=0)]
    psum x1 -> x0, waiting for transfers between devices: 172 us -> none  [shards(): column = lax.psum(local_grad, 'dp')]
    reduce_sum x0 -> x1, other arithmetic: none -> 15.8 us  [leaves_report(): mat_out = jax.lax.all_gather(body, group_axis).sum(axis=0)]
  transfers between devices with their start and end apart: 4 -> 4, of which waited for: 4 -> 4; matrix products, arithmetic and copies ran while one was open for 6% -> 2% of each run, Pallas kernels for 0% -> 0%
where the time goes in v1:
time: 913 us; the launch traced here: 912 us
  waiting for transfers between devices  801 us (88%)
  blocking collectives  39.7 us (4%)
  matrix products  35.7 us (4%)
  other arithmetic  20.3 us (2%)
  between operations  13.8 us (2%)
    all_gather x1, waiting for transfers between devices, leaves_report(): mat_out = jax.lax.all_gather(body, group_axis).sum(axis=0)  718 us
    reduce_scatter x1, waiting for transfers between devices, shards(): lax.psum_scatter(left_part / COUT, 'mp', scatter_dimension=1, tiled=True)  49.7 us
    psum x1, blocking collectives, shards(): small_total, large_total = lax.psum((small_sum, large_sum), ('dp', 'mp'))  39.7 us
    all_gather x1, waiting for transfers between devices, shards(): full_strip = lax.all_gather(rows_here, 'mp', axis=1, tiled=True)  24.2 us
  transfers between devices with their start and end apart: 4, of which 4 were waited for; matrix products, arithmetic and copies ran while one was open for 2% of the time, Pallas kernels for 0%

profile of v1, /device:TPU:0, one launch (start us, length us, event | category | flops | bytes accessed | tf_op | source)
XLA Modules:
  0.0 912.4 jit_solution(8548829471799162508)
XLA Ops:
  7.2 0.0 copy-start
  7.2 0.0 all-gather.6.cloned.1.call-start
  7.2 10.5 %multiply_reduce_fusion = (f32[]{:T(128)}, f32[3072,384]{1,0:T(8,128)}) fusion(f32[384]{0:T(512)} %param.11, f32[3072]{0:T(1024)} %param.10, bf16[1152,3072]{1,0:T(8,128)(2,1)} %param.6, bf16[1152,384]{1,0:T(8,128)(2,1)} %param.9), kind=kOutput, calls=%fused_computation | convolution fusion | flops 2722627584 | bytes 12695044 | tf_op jit(solution)/shard_map/dot_general | solution.py:25
  17.7 0.0 all-gather.6.cloned.1.call-update
  17.7 0.0 all-gather.4.cloned.1.call-start
  17.8 0.8 dynamic_slice.7
  18.5 718.4 %all-gather.6.cloned.1.call-done = f32[24576,384]{1,0:T(8,128)} async-done(((f32[3072,384]{1,0:T(8,128)}), f32[24576,384]{1,0:T(8,128)}) %all-gather.6.cloned.1.call-update) | async-done | bytes 37748752 | tf_op jit(solution)/shard_map/all_gather | solution.py:12
  736.9 0.0 copy-start.2
  736.9 15.8 %reduce_sum.27 = f32[3072,384]{1,0:T(8,128)} reduce(f32[8,3072,384]{2,1,0:T(8,128)} %bitcast.11, f32[]{:T(128)} %constant.5.clone.1), dimensions={0}, to_apply=%region_0.0 | reduce | flops 8257536 | bytes 42467332 | tf_op jit(solution)/shard_map/reduce_sum | solution.py:12
  752.8 0.0 copy-done.2
  752.8 2.5 multiply_reduce_fusion.1
  755.3 0.0 copy-start.1
  755.3 0.0 all-gather.4.cloned.1.call-update
  755.3 0.0 reduce-scatter.5.cloned.1.call-start
  755.4 24.2 %all-gather.4.cloned.1.call-done = f32[384,1536]{1,0:T(8,128)} async-done(((f32[384,384]{1,0:T(8,128)}), f32[384,1536]{1,0:T(8,128)}) %all-gather.4.cloned.1.call-update) | async-done | bytes 2359312 | tf_op jit(solution)/shard_map/all_gather | solution.py:40
  779.5 7.2 convolution_multiply_fusion.1
  786.8 0.0 reduce-scatter.5.cloned.1.call-update
  786.8 0.2 reduce-scatter.3.cloned.1.call-start
  787.0 0.0 copy-done.1
  787.0 11.0 %convolution_multiply_fusion = f32[384,3072]{1,0:T(8,128)} fusion(f32[384,384]{1,0:T(8,128)S(1)} %copy-done.1, f32[3072,384]{1,0:T(8,128)} %reduce_sum.27), kind=kOutput, calls=%fused_computation.1 | convolution fusion | flops 5436997632 | bytes 10027008 | tf_op jit(solution)/shard_map/dot_general | solution.py:32
  798.0 0.0 copy-start.3
  798.0 0.0 reduce-scatter.3.cloned.1.call-update
  798.0 0.0 copy-done
  798.0 0.6 copy-done.3
  798.7 7.1 fusion
  805.7 39.7 %all-reduce = (f32[1]{0:T(128)}, f32[1]{0:T(128)}) all-reduce(f32[1]{0:T(128)} %bitcast.2, f32[1]{0:T(128)} %bitcast.1), channel_id=1, replica_groups=mesh['dp'=8,'mp'=4] {'dp','mp'}, use_global_device_ids=true, to_apply=%region_6.0 | all-reduce | flops 2 | bytes 16 | tf_op jit(solution)/shard_map/psum | solution.py:57
  845.4 2.0 maximum_multiply_fusion
  847.4 8.8 reduce-scatter.5.cloned.1.call-done
  856.2 49.7 %reduce-scatter.3.cloned.1.call-done = f32[384,768]{1,0:T(8,128)} async-done(((f32[384,3072]{1,0:T(8,128)}), f32[384,768]{1,0:T(8,128)}) %reduce-scatter.3.cloned.1.call-update) | async-done | bytes 1179664 | tf_op jit(solution)/shard_map/reduce_scatter | solution.py:39
Async XLA Ops:
  7.2 790.8 %copy-start = (bf16[3072,384]{1,0:T(8,128)(2,1)S(1)}, bf16[3072,384]{1,0:T(8,128)(2,1)}, u32[]{:S(2)}) copy-start(bf16[3072,384]{1,0:T(8,128)(2,1)} %param.7) | copy-start | bytes 7077892
  7.2 729.8 %all-gather.6.cloned.1.call-start = ((), (), s32[]{:S(2)}) async-start(), calls=%async_computation.5 | async-start | bytes 42467328 | tf_op jit(solution)/shard_map/all_gather | solution.py:12
  17.7 761.8 %all-gather.4.cloned.1.call-start = ((), (), s32[]{:S(2)}) async-start(), calls=%async_computation.3 | async-start | bytes 2949120 | tf_op jit(solution)/shard_map/all_gather | solution.py:40
  736.9 15.8 %copy-start.2 = (f32[384]{0:T(512)S(1)}, f32[384]{0:T(512)}, u32[]{:S(2)}) copy-start(f32[384]{0:T(512)} %param.11) | copy-start | bytes 4612
  755.3 31.7 %copy-start.1 = (f32[384,384]{1,0:T(8,128)S(1)}, f32[384,384]{1,0:T(8,128)}, u32[]{:S(2)}) copy-start(f32[384,384]{1,0:T(8,128)} %get-tuple-element.7) | copy-start | bytes 1769476
  755.3 100.9 %reduce-scatter.5.cloned.1.call-start = ((), (), s32[]{:S(2)}) async-start(), calls=%async_computation.4 | async-start | bytes 2654208 | tf_op jit(solution)/shard_map/reduce_scatter | solution.py:41
  786.8 119.1 %reduce-scatter.3.cloned.1.call-start = ((), (), s32[]{:S(2)}) async-start(), calls=%async_computation.2 | async-start | bytes 5898240 | tf_op jit(solution)/shard_map/reduce_scatter | solution.py:39
  798.0 0.7 copy-start.3
Sparse Core Ops, SparseCore 0:
  17.8 719.0 all-gather.5
  755.5 24.0 all-gather.3
  786.9 69.2 reduce-scatter.4
  859.2 46.6 reduce-scatter.2

commit v2 on v0

--- a/solution.py
+++ b/solution.py
@@ -28,7 +28,15 @@
         preferred_element_type=jnp.float32,
     )
     left_factor = lax.psum_scatter(left_part / COUT, "mp", scatter_dimension=1, tiled=True)
-    full_strip = lax.all_gather(rows_here, "mp", axis=1, tiled=True)
+    n_parts = lax.axis_size("mp")
+    chunks = [(ii, (ii + 1) % n_parts) for ii in range(n_parts)]
+    y_new = [None] * n_parts
+    y_new[n_parts - 1] = rows_here
+    for i in range(n_parts - 2, -1, -1):
+        y_new[i] = lax.ppermute(y_new[i + 1], "mp", chunks)
+    even = jnp.concatenate(y_new, axis=1)
+    out_arr = (lax.axis_index("mp") + 1) * rows_here.shape[1]
+    full_strip = jnp.roll(even, shift=out_arr, axis=1)
     right_factor = lax.psum_scatter(
         lax.dot_general(
             full_strip,

time: 349 us -> 357 us (1.023)
  local copies, waits for them, and re-layouts: 1.44 us -> 6.25 us
  waiting for transfers between devices: 254 us -> 258 us
    ppermute x0 -> x3, waiting for transfers between devices: none -> 28.3 us  [shards(): y_new[i] = lax.ppermute(y_new[i + 1], 'mp', chunks)]
    all_gather x1 -> x0, waiting for transfers between devices: 23.2 us -> none  [shards(): full_strip = lax.all_gather(rows_here, 'mp', axis=1, tiled=True)]
    unnamed x8 -> x13, local copies, waits for them, and re-layouts: 0.66 us -> 5.4 us
  transfers between devices with their start and end apart: 4 -> 6, of which waited for: 4 -> 6; matrix products, arithmetic and copies ran while one was open for 6% -> 6% of each run, Pallas kernels for 0% -> 0%
where the time goes in v2:
time: 357 us
  waiting for transfers between devices  258 us (72%)
  blocking collectives  39.5 us (11%)
  matrix products  35.2 us (10%)
  between operations  13.8 us (4%)
  local copies, waits for them, and re-layouts  6.25 us (2%)
  other arithmetic  3.69 us (1%)
    psum x1, waiting for transfers between devices, shards(): column = lax.psum(local_grad, 'dp')  172 us
    reduce_scatter x1, waiting for transfers between devices, shards(): lax.psum_scatter(left_part / COUT, 'mp', scatter_dimension=1, tiled=True)  49.7 us
    psum x1, blocking collectives, shards(): small_total, large_total = lax.psum((small_sum, large_sum), ('dp', 'mp'))  39.5 us
    ppermute x3, waiting for transfers between devices, shards(): y_new[i] = lax.ppermute(y_new[i + 1], 'mp', chunks)  28.3 us
    dot_general x1, matrix products, shards(): lax.dot_general(rows_here, column, (((1,), (1,)), ((), ())), precision=la...  11 us
    dot_general x1, matrix products, shards(): lax.dot_general(patches, cotangent, (((0,), (0,)), ((), ())), preferred_e...  10.5 us
    reduce_scatter x1, waiting for transfers between devices, shards(): lax.psum_scatter(lax.dot_general(full_strip, rows_here, (((0,), (0,)), ((...  8.32 us
  transfers between devices with their start and end apart: 6, of which 6 were waited for; matrix products, arithmetic and copies ran while one was open for 6% of the time, Pallas kernels for 0%

profile of v2, /device:TPU:0, one launch (start us, length us, event | category | flops | bytes accessed | tf_op | source)
XLA Modules:
  0.0 356.8 jit_solution(11939947567226541536)
XLA Ops:
  7.2 0.0 copy-start
  7.2 0.0 all-reduce.3.cloned.1.call-start
  7.2 10.5 %multiply_reduce_fusion = (f32[]{:T(128)}, f32[3072,384]{1,0:T(8,128)}) fusion(f32[384]{0:T(512)} %param.11, f32[3072]{0:T(1024)} %param.10, bf16[1152,3072]{1,0:T(8,128)(2,1)} %param.6, bf16[1152,384]{1,0:T(8,128)(2,1)} %param.9), kind=kOutput, calls=%fused_computation | convolution fusion | flops 2722627584 | bytes 12695044 | tf_op jit(solution)/shard_map/dot_general | solution.py:16
  17.7 0.0 copy-start.1
  17.7 0.0 all-reduce.3.cloned.1.call-update
  17.7 0.0 reduce-scatter.5.cloned.1.call-start
  17.8 0.8 dynamic_slice.12
  18.6 171.7 %all-reduce.3.cloned.1.call-done = f32[3072,384]{1,0:T(8,128)} async-done(((f32[3072,384]{1,0:T(8,128)}), f32[3072,384]{1,0:T(8,128)}) %all-reduce.3.cloned.1.call-update) | async-done | bytes 4718608 | tf_op jit(solution)/shard_map/psum | solution.py:21
  190.2 0.0 copy-done.1
  190.2 1.9 multiply_reduce_fusion.1
  192.1 0.0 collective-permute-start
  192.2 9.3 %collective-permute-done = f32[384,384]{1,0:T(8,128)S(1)} collective-permute-done((f32[384,384]{1,0:T(8,128)S(1)}, f32[384,384]{1,0:T(8,128)S(1)}, u32[]{:S(2)}, u32[]{:S(2)}) %collective-permute-start) | collective-permute-done | bytes 589856 | tf_op jit(solution)/shard_map/ppermute | solution.py:36
  201.5 0.0 collective-permute-start.1
  201.5 9.4 %collective-permute-done.1 = f32[384,384]{1,0:T(8,128)} collective-permute-done((f32[384,384]{1,0:T(8,128)S(1)}, f32[384,384]{1,0:T(8,128)}, u32[]{:S(2)}, u32[]{:S(2)}) %collective-permute-start.1) | collective-permute-done | bytes 589856 | tf_op jit(solution)/shard_map/ppermute | solution.py:36
  210.9 0.0 collective-permute-start.2
  210.9 9.6 %collective-permute-done.2 = f32[384,384]{1,0:T(8,128)} collective-permute-done((f32[384,384]{1,0:T(8,128)}, f32[384,384]{1,0:T(8,128)}, u32[]{:S(2)}, u32[]{:S(2)}) %collective-permute-start.2) | collective-permute-done | bytes 589856 | tf_op jit(solution)/shard_map/ppermute | solution.py:36
  220.5 1.1 constant_dynamic-update-slice_fusion.7
  221.6 1.1 constant_dynamic-update-slice_fusion.6
  222.8 0.1 constant_dynamic-update-slice_fusion.5
  222.8 0.1 constant_dynamic-update-slice_fusion.4
  222.9 1.1 constant_dynamic-update-slice_fusion.3
  224.1 1.1 constant_dynamic-update-slice_fusion.2
  225.2 0.1 constant_dynamic-update-slice_fusion.1
  225.3 0.1 constant_dynamic-update-slice_fusion
  225.4 6.7 %convolution_multiply_fusion.1 = f32[1536,384]{1,0:T(8,128)} fusion(f32[384,384]{1,0:T(8,128)S(1)} %get-tuple-element.7, f32[384,3072]{1,0:T(8,128)S(1)} %constant_dynamic-update-slice_fusion, s32[]{:T(128)S(6)} %select_n.19), kind=kOutput, calls=%fused_computation.2 | convolution fusion | flops 2718498816 | bytes 5308420 | tf_op jit(solution)/shard_map/dot_general | solution.py:41
  232.1 0.0 reduce-scatter.5.cloned.1.call-update
  232.1 0.2 reduce-scatter.3.cloned.1.call-start
  232.3 11.0 %convolution_multiply_fusion = f32[384,3072]{1,0:T(8,128)} fusion(f32[384,384]{1,0:T(8,128)S(1)} %get-tuple-element.7, f32[3072,384]{1,0:T(8,128)} %all-reduce.3.cloned.1.call-done), kind=kOutput, calls=%fused_computation.1 | convolution fusion | flops 5436997632 | bytes 10027008 | tf_op jit(solution)/shard_map/dot_general | solution.py:23
  243.3 0.0 copy-start.2
  243.3 0.0 reduce-scatter.3.cloned.1.call-update
  243.3 0.0 copy-done
  243.3 0.6 copy-done.2
  243.9 7.1 %fusion = bf16[1152,384]{1,0:T(8,128)(2,1)} fusion(bf16[1152,3072]{1,0:T(8,128)(2,1)} %param.6, bf16[3072,384]{1,0:T(8,128)(2,1)S(1)} %copy-done, f32[384]{0:T(512)S(1)} %copy-done.2), kind=kOutput, calls=%fused_computation.4 | convolution fusion | flops 2718793728 | bytes 10323456 | tf_op jit(solution)/shard_map/dot_general | solution.py:11
  251.0 39.5 %all-reduce = (f32[1]{0:T(128)}, f32[1]{0:T(128)}) all-reduce(f32[1]{0:T(128)} %bitcast.1, f32[1]{0:T(128)} %bitcast), channel_id=1, replica_groups=mesh['dp'=8,'mp'=4] {'dp','mp'}, use_global_device_ids=true, to_apply=%region_6.7 | all-reduce | flops 2 | bytes 16 | tf_op jit(solution)/shard_map/psum | solution.py:56
  290.5 1.8 maximum_multiply_fusion
  292.3 8.3 %reduce-scatter.5.cloned.1.call-done = f32[192,384]{1,0:T(8,128)} async-done(((f32[1536,384]{1,0:T(8,128)}), f32[192,384]{1,0:T(8,128)}) %reduce-scatter.5.cloned.1.call-update) | async-done | bytes 294928 | tf_op jit(solution)/shard_map/reduce_scatter | solution.py:40
  300.6 49.7 %reduce-scatter.3.cloned.1.call-done = f32[384,768]{1,0:T(8,128)} async-done(((f32[384,3072]{1,0:T(8,128)}), f32[384,768]{1,0:T(8,128)}) %reduce-scatter.3.cloned.1.call-update) | async-done | bytes 1179664 | tf_op jit(solution)/shard_map/reduce_scatter | solution.py:30
Async XLA Ops:
  7.2 236.1 %copy-start = (bf16[3072,384]{1,0:T(8,128)(2,1)S(1)}, bf16[3072,384]{1,0:T(8,128)(2,1)}, u32[]{:S(2)}) copy-start(bf16[3072,384]{1,0:T(8,128)(2,1)} %param.7) | copy-start | bytes 7077892
  7.2 183.1 %all-reduce.3.cloned.1.call-start = ((), (), s32[]{:S(2)}) async-start(), calls=%async_computation.2 | async-start | bytes 9437184 | tf_op jit(solution)/shard_map/psum | solution.py:21
  17.7 172.5 %copy-start.1 = (f32[384]{0:T(512)S(1)}, f32[384]{0:T(512)}, u32[]{:S(2)}) copy-start(f32[384]{0:T(512)} %param.11) | copy-start | bytes 4612
  17.7 282.9 %reduce-scatter.5.cloned.1.call-start = ((), (), s32[]{:S(2)}) async-start(), calls=%async_computation.4 | async-start | bytes 2654208 | tf_op jit(solution)/shard_map/reduce_scatter | solution.py:40
  192.1 9.3 %collective-permute-start = (f32[384,384]{1,0:T(8,128)S(1)}, f32[384,384]{1,0:T(8,128)S(1)}, u32[]{:S(2)}, u32[]{:S(2)}) collective-permute-start(f32[384,384]{1,0:T(8,128)S(1)} %get-tuple-element.7), channel_id=1, source_target_pairs={{0,1},{1,2},{2,3},{3,0},{4,5},{5,6},{6,7},{7,4},{8,9},{9,10},{10,1... | collective-permute-start | bytes 1769480 | tf_op jit(solution)/shard_map/ppermute | solution.py:36
  201.5 9.4 %collective-permute-start.1 = (f32[384,384]{1,0:T(8,128)S(1)}, f32[384,384]{1,0:T(8,128)}, u32[]{:S(2)}, u32[]{:S(2)}) collective-permute-start(f32[384,384]{1,0:T(8,128)S(1)} %collective-permute-done), channel_id=1, source_target_pairs={{0,1},{1,2},{2,3},{3,0},{4,5},{5,6},{6,7},{7,4},{8,9},{9,10},{10,1... | collective-permute-start | bytes 1769480 | tf_op jit(solution)/shard_map/ppermute | solution.py:36
  210.9 9.6 %collective-permute-start.2 = (f32[384,384]{1,0:T(8,128)}, f32[384,384]{1,0:T(8,128)}, u32[]{:S(2)}, u32[]{:S(2)}) collective-permute-start(f32[384,384]{1,0:T(8,128)} %collective-permute-done.1), channel_id=1, source_target_pairs={{0,1},{1,2},{2,3},{3,0},{4,5},{5,6},{6,7},{7,4},{8,9},{9,10},{10,1... | collective-permute-start | bytes 1769480 | tf_op jit(solution)/shard_map/ppermute | solution.py:36
  232.1 118.2 %reduce-scatter.3.cloned.1.call-start = ((), (), s32[]{:S(2)}) async-start(), calls=%async_computation.3 | async-start | bytes 5898240 | tf_op jit(solution)/shard_map/reduce_scatter | solution.py:30
  243.3 0.7 copy-start.2
Sparse Core Ops, SparseCore 0:
  17.8 172.3 all-reduce.2
  232.2 68.3 reduce-scatter.4
  303.7 46.4 reduce-scatter.2
